TPU v7x, 32 devices: a whole 2x2x4 slice. The times are simulated.
32 devices in a mesh: shot: 8 (over y, x, core), pair: 4 (over z).
Axes of the slice: x: 2, y: 2, z: 4, core: 2. Of those that a mesh axis runs over, the one named last changes fastest.
Arguments:
- spectra: bfloat16 [2, 128, 128, 1024], P(None, 'shot', None, 'pair'), may hold values from -6 to 6
- shot_weight: float32 [128], P('shot'), may hold values from 0.5 to 2
Outputs:
- virtual_gather: bfloat16 [2, 128, 1024, 1024], P(None, 'shot', 'pair')
All inputs are finite; a program needn't handle non-finite values.
Results may differ from a plain program's by a relative error of at most 0.0054.
Values may be sent and summed in bfloat16 or wider, within the bound.
A program may use at most 128 MiB of HBM per device.

v0:
```python
import jax
import jax.numpy as jnp
from jax import lax
from jax.sharding import PartitionSpec as P


def gram_block(row_data, column_data, factor):
    swapped = jnp.stack([-row_data[1], row_data[0]])
    left_side = jnp.stack([row_data, swapped])
    product = jnp.einsum(
        "ocsfa,csfb->ofab", left_side, column_data, preferred_element_type=jnp.float32
    )
    return product * factor


def shards(spectra, shot_weight):
    scaled = (spectra.astype(jnp.float32) * shot_weight[None, :, None, None]).astype(jnp.bfloat16)
    by_freq = lax.all_to_all(scaled, "shot", split_axis=2, concat_axis=1, tiled=True)
    total_shots = by_freq.shape[1]
    factor = total_shots ** (-0.5)
    full_rows = gram_block(by_freq, lax.all_gather(by_freq, "pair", axis=3, tiled=True), factor)
    return full_rows.astype(jnp.bfloat16)


def solution(mesh):
    return jax.shard_map(
        shards,
        mesh=mesh,
        in_specs=(P(None, "shot", None, "pair"), P("shot")),
        out_specs=P(None, "shot", "pair", None),
        check_vma=False,
    )
```

profile of v0, /device:TPU:0, one launch (start us, length us, event | category | flops | bytes accessed | tf_op | source)
XLA Modules:
  0.0 237.3 jit_solution(6709182819881926623)
XLA Ops:
  6.5 0.0 all-gather.2.cloned.1.call-start
  6.5 2.8 %multiply_convert_fusion = bf16[2,16,128,256]{3,1,0,2:T(8,128)(2,1)S(1)} fusion(bf16[2,16,128,256]{3,2,1,0:T(8,128)(2,1)} %param.2, f32[16]{0:T(128)} %param.3), kind=kLoop, calls=%fused_computation.7 | loop fusion | flops 3145728 | bytes 4194368 | tf_op jit(solution)/shard_map/convert_element_type | solution.py:17
  9.4 31.6 %all_to_all.18 = bf16[2,16,128,256]{3,1,0,2:T(8,128)(2,1)S(1)} all-to-all(bf16[2,16,128,256]{3,1,0,2:T(8,128)(2,1)S(1)} %multiply_convert_fusion), channel_id=1, replica_groups=mesh['shot'=8,'pair'=4] {'shot'}, dimensions={2} | all-to-all | bytes 4194304 | tf_op jit(solution)/shard_map/all_to_all | solution.py:18
  40.9 2.5 %copy.20 = bf16[2,8,16,16,256]{4,3,2,1,0:T(8,128)(2,1)} copy(bf16[2,8,16,16,256]{4,2,0,3,1:T(8,128)(2,1)S(1)} %bitcast.25) | data formatting | bytes 4194304 | tf_op jit(solution)/shard_map/all_to_all | solution.py:18
  43.4 4.6 %copy.21 = bf16[2,128,16,256]{1,3,0,2:T(8,128)(2,1)} copy(bf16[2,128,16,256]{3,2,1,0:T(8,128)(2,1)} %bitcast.28) | data formatting | bytes 4194304 | tf_op jit(solution)/shard_map/all_to_all | solution.py:18
  48.0 0.0 all-gather.2.cloned.1.call-update
  48.0 1.6 copy.22
  49.6 1.2 copy.19
  50.8 0.1 slice_negate_fusion
  50.9 0.0 copy-start
  50.9 0.6 copy.23
  51.5 0.6 copy.24
  52.1 1.5 maximum_bitcast_fusion
  53.6 143.5 %all-gather.2.cloned.1.call-done = bf16[2,128,16,1024]{1,3,0,2:T(8,128)(2,1)} async-done(((bf16[2,128,16,256]{1,3,0,2:T(8,128)(2,1)}), bf16[2,128,16,1024]{1,3,0,2:T(8,128)(2,1)}) %all-gather.2.cloned.1.call-update) | async-done | bytes 8388624 | tf_op jit(solution)/shard_map/all_gather | solution.py:21
  197.2 0.0 copy-done
  197.2 11.0 %fusion.1 = bf16[2,16,256,1024]{2,3,0,1:T(8,128)(2,1)} fusion(bf16[2,128,16,1024]{1,3,0,2:T(8,128)(2,1)} %all-gather.2.cloned.1.call-done, bf16[1,2,128,16,256]{4,2,1,0,3:T(8,128)(2,1)} %maximum_bitcast_fusion, bf16[1,2,128,16,256]{4,2,1,0,3:T(8,128)(2,1)S(1)} %bitcast.31), kind=kOutput, calls=%fused_computation.2 | convolution fusion | flops 4320133120 | bytes 29360128 | tf_op jit(solution)/shard_map/ocsfa,csfb->ofab/dot_general | solution.py:10
  208.1 22.4 %copy.25 = bf16[2,16,256,1024]{3,2,1,0:T(8,128)(2,1)} copy(bf16[2,16,256,1024]{2,3,0,1:T(8,128)(2,1)} %fusion.1) | data formatting | bytes 33554432 | tf_op jit(solution)/shard_map/convert_element_type | solution.py:22
Async XLA Ops:
  6.5 190.6 %all-gather.2.cloned.1.call-start = ((), (), s32[]{:S(2)}) async-start(), calls=%async_computation.1 | async-start | bytes 10485760 | tf_op jit(solution)/shard_map/all_gather | solution.py:21
  50.9 146.2 %copy-start = (bf16[2,8,16,16,256]{4,2,1,0,3:T(8,128)(2,1)S(1)}, bf16[2,8,16,16,256]{4,2,1,0,3:T(8,128)(2,1)}, u32[]{:S(2)}) copy-start(bf16[2,8,16,16,256]{4,2,1,0,3:T(8,128)(2,1)} %copy.22) | copy-start | bytes 6291460
Sparse Core Ops, SparseCore 0:
  48.1 148.9 all-gather.1
where the time goes:
time: 238 us; the launch traced here: 237 us
  waiting for transfers between devices  144 us (61%)
  local copies, waits for them, and re-layouts  33.4 us (14%)
  blocking collectives  31.6 us (13%)
  between operations  13.4 us (6%)
  matrix products  11 us (5%)
  other arithmetic  4.48 us (2%)
    all_gather x1, waiting for transfers between devices, shards(): lax.all_gather(by_freq, 'pair', axis=3, tiled=True)  144 us
    all_to_all x1, blocking collectives, shards(): lax.all_to_all(scaled, 'shot', split_axis=2, concat_axis=1, tiled=True)  31.6 us
    convert_element_type x1, local copies, waits for them, and re-layouts, shards(): return full_rows.astype(jnp.bfloat16)  22.4 us
    dot_general x1, matrix products, gram_block(): jnp.einsum('ocsfa,csfb->ofab', left_side, column_data, preferred_element_...  11 us
    all_to_all x4, local copies, waits for them, and re-layouts, shards(): lax.all_to_all(scaled, 'shot', split_axis=2, concat_axis=1, tiled=True)  9.82 us
  transfers between devices with their start and end apart: 1, of which 1 were waited for; matrix products, arithmetic and copies ran while one was open for 2% of the time, Pallas kernels for 0%

commit v1 on v0

v1 whole, which is shorter than its diff:
```python
import functools

import jax
import jax.numpy as jnp
from jax import lax
from jax.experimental import pallas as pl
from jax.experimental.pallas import tpu as pltpu
from jax.sharding import PartitionSpec as P

MESH = pl.DeviceIdType.MESH


def meet(me, step, count):
    out, bit = 0, 1
    while bit < count:
        out = out + ((me // bit + step // bit) % 2) * bit
        bit *= 2
    return out


def gather_kernel(ns, np_, x_ref, g_ref, a2a_sem, up_sem, down_sem, recv_sem, own_sem):
    s, p = lax.axis_index("shot"), lax.axis_index("pair")
    has_up, has_down = p < np_ - 1, p > 0

    barrier = pltpu.get_barrier_semaphore()

    def hello(t, carry):
        pl.semaphore_signal(barrier, inc=1, device_id=(meet(s, t, ns), p), device_id_type=MESH)
        return carry

    lax.fori_loop(1, ns, hello, 0)

    @pl.when(has_up)
    def _():
        pl.semaphore_signal(barrier, inc=1, device_id=(s, p + 1), device_id_type=MESH)

    @pl.when(has_down)
    def _():
        pl.semaphore_signal(barrier, inc=1, device_id=(s, p - 1), device_id_type=MESH)

    pl.semaphore_wait(barrier, ns - 1 + has_up.astype(jnp.int32) + has_down.astype(jnp.int32))

    def up(q, j, src):
        return pltpu.make_async_remote_copy(
            src_ref=src, dst_ref=g_ref.at[q, j], send_sem=up_sem.at[q, j],
            recv_sem=recv_sem.at[q, j], device_id=(s, p + 1), device_id_type=MESH)

    def down(q, j, src):
        return pltpu.make_async_remote_copy(
            src_ref=src, dst_ref=g_ref.at[q, j], send_sem=down_sem.at[q, j],
            recv_sem=recv_sem.at[q, j], device_id=(s, p - 1), device_id_type=MESH)

    def exchange(t):
        j = meet(s, t, ns)
        return pltpu.make_async_remote_copy(
            src_ref=x_ref.at[j], dst_ref=g_ref.at[p, s], send_sem=a2a_sem.at[t],
            recv_sem=recv_sem.at[p, s], device_id=(j, p), device_id_type=MESH)

    def arrived(q, j):
        pltpu.make_async_copy(g_ref.at[q, j], g_ref.at[q, j], recv_sem.at[q, j]).wait()

    own = pltpu.make_async_copy(x_ref.at[s], g_ref.at[p, s], own_sem)

    @pl.when(has_up)
    def _():
        up(p, s, x_ref.at[s]).start()

    @pl.when(has_down)
    def _():
        down(p, s, x_ref.at[s]).start()

    def send(t, carry):
        exchange(t).start()
        return carry

    lax.fori_loop(1, ns, send, 0)
    own.start()

    def first(t, carry):
        j = meet(s, t, ns)
        arrived(p, j)

        @pl.when(has_up)
        def _():
            up(p, j, g_ref.at[p, j]).start()

        @pl.when(has_down)
        def _():
            down(p, j, g_ref.at[p, j]).start()

        return carry

    lax.fori_loop(1, ns, first, 0)

    def relay(i, carry):
        r, j = i // ns, meet(s, i % ns, ns)

        @pl.when(p >= r)
        def _():
            arrived(p - r, j)

            @pl.when(has_up)
            def _():
                up(p - r, j, g_ref.at[p - r, j]).start()

        @pl.when(p + r < np_)
        def _():
            arrived(p + r, j)

            @pl.when(has_down)
            def _():
                down(p + r, j, g_ref.at[p + r, j]).start()

        return carry

    lax.fori_loop(ns, np_ * ns, relay, 0)

    own.wait()

    def exchanged(t, carry):
        exchange(t).wait_send()
        return carry

    lax.fori_loop(1, ns, exchanged, 0)

    def sent(i, carry):
        q, j = i // ns, i % ns

        @pl.when(has_up & (q <= p))
        def _():
            up(q, j, g_ref.at[q, j]).wait_send()

        @pl.when(has_down & (q >= p))
        def _():
            down(q, j, g_ref.at[q, j]).wait_send()

        return carry

    lax.fori_loop(0, np_ * ns, sent, 0)


def gram_kernel(factor, g_ref, o_ref):
    parts, width = g_ref.shape[0], g_ref.shape[-1]
    rows = g_ref[lax.axis_index("pair"), :, 0]
    swapped = jnp.concatenate([-rows[:, 1:2], rows[:, 0:1]], axis=1)
    left = jnp.concatenate([rows.reshape(-1, width), swapped.reshape(-1, width)], axis=1)
    for q in range(parts):
        right = g_ref[q, :, 0].reshape(-1, width)
        product = lax.dot_general(left, right, (((0,), (0,)), ((), ())), preferred_element_type=jnp.float32)
        product = (product * factor).astype(o_ref.dtype)
        o_ref[0, 0, :, q * width:(q + 1) * width] = product[:width]
        o_ref[1, 0, :, q * width:(q + 1) * width] = product[width:]


def gram(gathered, factor):
    np_, ns, bins, _, depth, width = gathered.shape
    if width % 128 == 0:
        return pl.pallas_call(
            functools.partial(gram_kernel, factor),
            grid=(bins,),
            in_specs=[pl.BlockSpec((np_, ns, 1, 2, depth, width), lambda f: (0, 0, f, 0, 0, 0))],
            out_specs=pl.BlockSpec((2, 1, width, np_ * width), lambda f: (0, f, 0, 0)),
            out_shape=jax.ShapeDtypeStruct((2, bins, width, np_ * width), jnp.bfloat16),
        )(gathered)
    rows = lax.dynamic_index_in_dim(gathered, lax.axis_index("pair"), 0, keepdims=False)
    left = jnp.stack([rows, jnp.stack([-rows[:, :, 1], rows[:, :, 0]], axis=2)])
    product = jnp.einsum("ojfcsa,qjfcsb->ofaqb", left, gathered, preferred_element_type=jnp.float32)
    return (product * factor).astype(jnp.bfloat16).reshape(2, bins, width, np_ * width)


def shards(ns, np_, spectra, shot_weight):
    _, depth, freqs, width = spectra.shape
    bins = freqs // ns
    scaled = (spectra.astype(jnp.float32) * shot_weight[None, :, None, None]).astype(jnp.bfloat16)
    outgoing = scaled.transpose(2, 0, 1, 3).reshape(ns, bins, 2, depth, width)
    gathered = pl.pallas_call(
        functools.partial(gather_kernel, ns, np_),
        out_shape=jax.ShapeDtypeStruct((np_, *outgoing.shape), jnp.bfloat16),
        in_specs=[pl.BlockSpec(memory_space=pl.ANY)],
        out_specs=pl.BlockSpec(memory_space=pl.ANY),
        scratch_shapes=[
            pltpu.SemaphoreType.DMA((ns,)),
            pltpu.SemaphoreType.DMA((np_, ns)),
            pltpu.SemaphoreType.DMA((np_, ns)),
            pltpu.SemaphoreType.DMA((np_, ns)),
            pltpu.SemaphoreType.DMA,
        ],
        compiler_params=pltpu.CompilerParams(collective_id=0, has_side_effects=True),
    )(outgoing)
    return gram(gathered, (depth * ns) ** -0.5)


def solution(mesh):
    return jax.shard_map(
        functools.partial(shards, mesh.shape["shot"], mesh.shape["pair"]),
        mesh=mesh,
        in_specs=(P(None, "shot", None, "pair"), P("shot")),
        out_specs=P(None, "shot", "pair", None),
        check_vma=False,
    )
```

time: 238 us -> 165 us (0.69)
  Pallas kernels: 0 us -> 160 us
  waiting for transfers between devices: 144 us -> 0 us
  blocking collectives: 31.6 us -> 0 us
  local copies, waits for them, and re-layouts: 33.4 us -> 2.51 us
  between operations: 13.4 us -> 0.02 us
  matrix products: 11 us -> 0 us
    pallas_call x0 -> x2, Pallas kernels: none -> 160 us  [the longest x1 143 us: shards(): pl.pallas_call(functools.partial(gather_kernel, ns, np_), out_shape=jax.S...]
    all_gather x1 -> x0, waiting for transfers between devices: 144 us -> none  [shards(): lax.all_gather(by_freq, 'pair', axis=3, tiled=True)]
    all_to_all x1 -> x0, blocking collectives: 31.6 us -> none  [shards(): lax.all_to_all(scaled, 'shot', split_axis=2, concat_axis=1, tiled=True)]
    convert_element_type x1 -> x0, local copies, waits for them, and re-layouts: 22.4 us -> none  [shards(): return full_rows.astype(jnp.bfloat16)]
    dot_general x1 -> x0, matrix products: 11 us -> none  [gram_block(): jnp.einsum('ocsfa,csfb->ofab', left_side, column_data, preferred_element_...]
    all_to_all x4 -> x0, local copies, waits for them, and re-layouts: 9.82 us -> none  [shards(): lax.all_to_all(scaled, 'shot', split_axis=2, concat_axis=1, tiled=True)]
    convert_element_type x1 -> x0, other arithmetic: 2.84 us -> none  [shards(): (spectra.astype(jnp.float32) * shot_weight[None, :, None, None]).astype(j...]
    transpose x0 -> x1, other arithmetic: none -> 2.62 us  [shards(): outgoing = scaled.transpose(2, 0, 1, 3).reshape(ns, bins, 2, depth, width)]
  transfers between devices with their start and end apart: 1 -> 0, of which waited for: 1 -> 0; matrix products, arithmetic and copies ran while one was open for 2% -> 0% of each run, Pallas kernels for 0% -> 0%
where the time goes in v1:
time: 165 us
  Pallas kernels  160 us (97%)
  other arithmetic  2.62 us (2%)
  local copies, waits for them, and re-layouts  2.51 us (2%)
    pallas_call x1, Pallas kernels, shards(): pl.pallas_call(functools.partial(gather_kernel, ns, np_), out_shape=jax.S...  143 us
    pallas_call x1, Pallas kernels, gram(): pl.pallas_call(functools.partial(gram_kernel, factor), grid=(bins,), in_s...  16.6 us

profile of v1, /device:TPU:0, one launch (start us, length us, event | category | flops | bytes accessed | tf_op | source)
XLA Modules:
  0.0 164.8 jit_solution(7727378996523386796)
XLA Ops:
  0.0 2.6 %fusion = bf16[128,2,16,256]{3,0,2,1:T(8,128)(2,1)S(1)} fusion(bf16[2,16,128,256]{3,2,1,0:T(8,128)(2,1)} %param.2, f32[16]{0:T(128)} %param.3), kind=kLoop, calls=%fused_computation.1 | loop fusion | flops 3145728 | bytes 4194368 | tf_op jit(solution)/shard_map/transpose | solution.py:175
  2.6 2.5 %copy.3 = bf16[128,2,16,256]{3,2,1,0:T(8,128)(2,1)} copy(bf16[128,2,16,256]{3,0,2,1:T(8,128)(2,1)S(1)} %fusion) | data formatting | bytes 4194304 | tf_op jit(solution)/shard_map/transpose | solution.py:175
  5.1 143.1 %shard_map.28.g_ref = bf16[4,8,16,2,16,256]{5,4,3,2,1,0:T(8,128)(2,1)} custom-call(bf16[8,16,2,16,256]{4,3,2,1,0:T(8,128)(2,1)} %bitcast.3), custom_call_target="tpu_custom_call" | custom-call | tf_op jit(solution)/shard_map/pallas_call | solution.py:176
  148.2 16.6 %shard_map.29 = bf16[2,16,256,1024]{3,2,1,0:T(8,128)(2,1)} custom-call(bf16[4,8,16,2,16,256]{5,4,3,2,1,0:T(8,128)(2,1)} %shard_map.28.g_ref), custom_call_target="tpu_custom_call" | custom-call | tf_op jit(solution)/shard_map/pallas_call | solution.py:158

commit v2 on v1

--- a/solution.py
+++ b/solution.py
@@ -18,8 +18,28 @@
     return out
 
 
-def gather_kernel(ns, np_, x_ref, g_ref, a2a_sem, up_sem, down_sem, recv_sem, own_sem):
+def put_left(f, p, g_ref, left_ref):
+    width = g_ref.shape[-1]
+    rows = g_ref[p, :, f]
+    swapped = jnp.concatenate([-rows[:, 1:2], rows[:, 0:1]], axis=1)
+    left = jnp.concatenate([rows.reshape(-1, width), swapped.reshape(-1, width)], axis=1)
+    left_ref[f] = left.T
+
+
+def block_product(f, q, g_ref, left_ref, factor):
+    width = g_ref.shape[-1]
+    right = g_ref[q, :, f].reshape(-1, width)
+    return (jnp.dot(left_ref[f], right, preferred_element_type=jnp.float32) * factor).astype(jnp.bfloat16)
+
+
+def gather_kernel(ns, np_, factor, fused, x_ref, g_ref, *rest):
+    if fused:
+        left_ref, o_ref, a2a_sem, up_sem, down_sem, recv_sem, own_sem = rest
+    else:
+        a2a_sem, up_sem, down_sem, recv_sem, own_sem = rest
     s, p = lax.axis_index("shot"), lax.axis_index("pair")
+    bins, width = g_ref.shape[2], g_ref.shape[-1]
+    share = -(-bins // ns)
     has_up, has_down = p < np_ - 1, p > 0
 
     barrier = pltpu.get_barrier_semaphore()
@@ -92,6 +112,33 @@
 
     lax.fori_loop(1, ns, first, 0)
 
+    own.wait()
+
+    def multiply(f, q):
+        product = block_product(f, q, g_ref, left_ref, factor)
+        columns = pl.ds(pl.multiple_of(q * width, width), width)
+        o_ref[0, f, :, columns] = product[:width]
+        o_ref[1, f, :, columns] = product[width:]
+
+    def compute(r, t):
+        def one_bin(f, carry):
+            @pl.when(r == 0)
+            def _():
+                put_left(f, p, g_ref, left_ref)
+                multiply(f, p)
+
+            @pl.when((r > 0) & (p >= r))
+            def _():
+                multiply(f, p - r)
+
+            @pl.when((r > 0) & (p + r < np_))
+            def _():
+                multiply(f, p + r)
+
+            return carry
+
+        lax.fori_loop(jnp.minimum(t * share, bins), jnp.minimum((t + 1) * share, bins), one_bin, 0)
+
     def relay(i, carry):
         r, j = i // ns, meet(s, i % ns, ns)
 
@@ -111,11 +158,11 @@
             def _():
                 down(p + r, j, g_ref.at[p + r, j]).start()
 
+        if fused:
+            compute(r - 1, i % ns)
         return carry
 
     lax.fori_loop(ns, np_ * ns, relay, 0)
-
-    own.wait()
 
     def exchanged(t, carry):
         exchange(t).wait_send()
@@ -139,29 +186,64 @@
     lax.fori_loop(0, np_ * ns, sent, 0)
 
 
-def gram_kernel(factor, g_ref, o_ref):
-    parts, width = g_ref.shape[0], g_ref.shape[-1]
-    rows = g_ref[lax.axis_index("pair"), :, 0]
-    swapped = jnp.concatenate([-rows[:, 1:2], rows[:, 0:1]], axis=1)
-    left = jnp.concatenate([rows.reshape(-1, width), swapped.reshape(-1, width)], axis=1)
-    for q in range(parts):
-        right = g_ref[q, :, 0].reshape(-1, width)
-        product = lax.dot_general(left, right, (((0,), (0,)), ((), ())), preferred_element_type=jnp.float32)
-        product = (product * factor).astype(o_ref.dtype)
-        o_ref[0, 0, :, q * width:(q + 1) * width] = product[:width]
-        o_ref[1, 0, :, q * width:(q + 1) * width] = product[width:]
+def finish_kernel(np_, factor, g_ref, left_ref, o_ref, out_ref, last_ref, done_sem, last_sem):
+    p = lax.axis_index("pair")
+    bins, width = g_ref.shape[2], g_ref.shape[-1]
+    at_end = (p == 0) | (p == np_ - 1)
+    q = np_ - 1 - p
+
+    def whole(f):
+        return pltpu.make_async_copy(o_ref.at[:, f], out_ref.at[:, f], done_sem.at[f])
+
+    def most(f):
+        columns = pl.ds(pl.multiple_of(jnp.where(p == 0, 0, width), width), (np_ - 1) * width)
+        return pltpu.make_async_copy(o_ref.at[:, f, :, columns], out_ref.at[:, f, :, columns], done_sem.at[f])
+
+    def last(f):
+        columns = pl.ds(pl.multiple_of(q * width, width), width)
+        return pltpu.make_async_copy(last_ref.at[:, f], out_ref.at[:, f, :, columns], last_sem.at[f])
+
+    @pl.when(at_end)
+    def _():
+        for f in range(bins):
+            most(f).start()
+        for f in range(bins):
+            product = block_product(f, q, g_ref, left_ref, factor)
+            last_ref[0, f] = product[:width]
+            last_ref[1, f] = product[width:]
+            if f > 0:
+                last(f - 1).start()
+        last(bins - 1).start()
+        for f in range(bins):
+            most(f).wait()
+            last(f).wait()
+
+    @pl.when(jnp.logical_not(at_end))
+    def _():
+        for f in range(bins):
+            whole(f).start()
+        for f in range(bins):
+            whole(f).wait()
+
+
+def finish(np_, factor, gathered, left, products):
+    _, bins, width, columns = products.shape
+    return pl.pallas_call(
+        functools.partial(finish_kernel, np_, factor),
+        out_shape=jax.ShapeDtypeStruct(products.shape, jnp.bfloat16),
+        in_specs=[pl.BlockSpec(memory_space=pltpu.VMEM)] * 3,
+        out_specs=pl.BlockSpec(memory_space=pl.ANY),
+        scratch_shapes=[
+            pltpu.VMEM((2, bins, width, width), jnp.bfloat16),
+            pltpu.SemaphoreType.DMA((bins,)),
+            pltpu.SemaphoreType.DMA((bins,)),
+        ],
+        compiler_params=pltpu.CompilerParams(vmem_limit_bytes=16 * 2**20),
+    )(*(pltpu.with_memory_space_constraint(a, pltpu.VMEM) for a in (gathered, left, products)))
 
 
 def gram(gathered, factor):
     np_, ns, bins, _, depth, width = gathered.shape
-    if width % 128 == 0:
-        return pl.pallas_call(
-            functools.partial(gram_kernel, factor),
-            grid=(bins,),
-            in_specs=[pl.BlockSpec((np_, ns, 1, 2, depth, width), lambda f: (0, 0, f, 0, 0, 0))],
-            out_specs=pl.BlockSpec((2, 1, width, np_ * width), lambda f: (0, f, 0, 0)),
-            out_shape=jax.ShapeDtypeStruct((2, bins, width, np_ * width), jnp.bfloat16),
-        )(gathered)
     rows = lax.dynamic_index_in_dim(gathered, lax.axis_index("pair"), 0, keepdims=False)
     left = jnp.stack([rows, jnp.stack([-rows[:, :, 1], rows[:, :, 0]], axis=2)])
     product = jnp.einsum("ojfcsa,qjfcsb->ofaqb", left, gathered, preferred_element_type=jnp.float32)
@@ -173,11 +255,17 @@
     bins = freqs // ns
     scaled = (spectra.astype(jnp.float32) * shot_weight[None, :, None, None]).astype(jnp.bfloat16)
     outgoing = scaled.transpose(2, 0, 1, 3).reshape(ns, bins, 2, depth, width)
-    gathered = pl.pallas_call(
-        functools.partial(gather_kernel, ns, np_),
-        out_shape=jax.ShapeDtypeStruct((np_, *outgoing.shape), jnp.bfloat16),
+    factor = (depth * ns) ** -0.5
+    fused = width % 128 == 0
+    shapes = [(np_, ns, bins, 2, depth, width)]
+    if fused:
+        shapes += [(bins, 2 * width, ns * 2 * depth), (2, bins, width, np_ * width)]
+    place = pltpu.VMEM if fused else pl.ANY
+    results = pl.pallas_call(
+        functools.partial(gather_kernel, ns, np_, factor, fused),
+        out_shape=[pltpu.VMEM(n, jnp.bfloat16) if fused else jax.ShapeDtypeStruct(n, jnp.bfloat16) for n in shapes],
         in_specs=[pl.BlockSpec(memory_space=pl.ANY)],
-        out_specs=pl.BlockSpec(memory_space=pl.ANY),
+        out_specs=[pl.BlockSpec(memory_space=place)] * len(shapes),
         scratch_shapes=[
             pltpu.SemaphoreType.DMA((ns,)),
             pltpu.SemaphoreType.DMA((np_, ns)),
@@ -185,9 +273,12 @@
             pltpu.SemaphoreType.DMA((np_, ns)),
             pltpu.SemaphoreType.DMA,
         ],
-        compiler_params=pltpu.CompilerParams(collective_id=0, has_side_effects=True),
+        compiler_params=pltpu.CompilerParams(
+            collective_id=0, has_side_effects=True, vmem_limit_bytes=16 * 2**20),
     )(outgoing)
-    return gram(gathered, (depth * ns) ** -0.5)
+    if fused:
+        return finish(np_, factor, *results)
+    return gram(results[0], factor)
 
 
 def solution(mesh):

time: 165 us -> 154 us (0.933)
  Pallas kernels: 160 us -> 150 us
    pallas_call x2, Pallas kernels: 160 us -> 150 us  [the longest x1 144 us: shards(): pl.pallas_call(functools.partial(gather_kernel, ns, np_, factor, fused),...]
where the time goes in v2:
time: 154 us; the launch traced here: 153 us
  Pallas kernels  150 us (97%)
  other arithmetic  2.62 us (2%)
    pallas_call x1, Pallas kernels, shards(): pl.pallas_call(functools.partial(gather_kernel, ns, np_, factor, fused),...  144 us
    pallas_call x1, Pallas kernels, finish(): pl.pallas_call(functools.partial(finish_kernel, np_, factor), out_shape=j...  6.09 us

profile of v2, /device:TPU:0, one launch (start us, length us, event | category | flops | bytes accessed | tf_op | source)
XLA Modules:
  0.0 153.4 jit_solution(17024798394119503509)
XLA Ops:
  0.0 2.6 %fusion = bf16[128,2,16,256]{3,0,2,1:T(8,128)(2,1)S(1)} fusion(bf16[2,16,128,256]{3,2,1,0:T(8,128)(2,1)} %param.2, f32[16]{0:T(128)} %param.3), kind=kLoop, calls=%fused_computation.1 | loop fusion | flops 3145728 | bytes 4194368 | tf_op jit(solution)/shard_map/transpose | solution.py:257
  2.6 1.2 copy.3
  3.8 143.5 %shard_map.28 = (bf16[4,8,16,2,16,256]{5,4,3,2,1,0:T(8,128)(2,1)S(1)}, bf16[16,512,256]{2,1,0:T(8,128)(2,1)S(1)}, bf16[2,16,256,1024]{3,2,1,0:T(8,128)(2,1)S(1)}) custom-call(bf16[8,16,2,16,256]{4,3,2,1,0:T(8,128)(2,1)S(1)} %bitcast.3), custom_call_target="tpu_custom_call" | custom-call | tf_op jit(solution)/shard_map/pallas_call | solution.py:264
  147.3 6.1 %shard_map.29 = bf16[2,16,256,1024]{3,2,1,0:T(8,128)(2,1)} custom-call(bf16[4,8,16,2,16,256]{5,4,3,2,1,0:T(8,128)(2,1)S(1)} %get-tuple-element.8.g_ref, bf16[16,512,256]{2,1,0:T(8,128)(2,1)S(1)} %get-tuple-element.9.left_ref, bf16[2,16,256,1024]{3,2,1,0:T(8,128)(2,1)S(1)} %get-tuple-element.10.o_ref), custom_call_target="tpu_custom_call" | custom-call | tf_op jit(solution)/shard_map/pallas_call | solution.py:231

commit v3 on v2

--- a/solution.py
+++ b/solution.py
@@ -32,11 +32,26 @@
     return (jnp.dot(left_ref[f], right, preferred_element_type=jnp.float32) * factor).astype(jnp.bfloat16)
 
 
-def gather_kernel(ns, np_, factor, fused, x_ref, g_ref, *rest):
+def prepare(t, j, raw_ref, weight_ref, wide_ref, x_ref):
+    _, _, depth, bins, width = raw_ref.shape
+    for c in range(2):
+        for k in range(depth):
+            scaled = raw_ref[t, c, k].astype(jnp.float32) * weight_ref[k]
+            for h in range(width // 128):
+                wide_ref[h, pl.ds((c * depth + k) * bins, bins), :] = scaled[:, h * 128:(h + 1) * 128]
+    for c in range(2):
+        for f in range(bins):
+            for h in range(width // 128):
+                shots = wide_ref[h, pl.ds(c * depth * bins + f, depth, stride=bins), :]
+                x_ref[j, f, c, :, h * 128:(h + 1) * 128] = shots.astype(jnp.bfloat16)
+
+
+def gather_kernel(ns, np_, factor, fused, *refs):
     if fused:
-        left_ref, o_ref, a2a_sem, up_sem, down_sem, recv_sem, own_sem = rest
+        spectra_ref, weight_ref, g_ref, left_ref, o_ref, x_ref, raw_ref, wide_ref, load_sem, *sems = refs
     else:
-        a2a_sem, up_sem, down_sem, recv_sem, own_sem = rest
+        x_ref, g_ref, *sems = refs
+    a2a_sem, up_sem, down_sem, recv_sem, own_sem = sems
     s, p = lax.axis_index("shot"), lax.axis_index("pair")
     bins, width = g_ref.shape[2], g_ref.shape[-1]
     share = -(-bins // ns)
@@ -57,6 +72,19 @@
     @pl.when(has_down)
     def _():
         pl.semaphore_signal(barrier, inc=1, device_id=(s, p - 1), device_id_type=MESH)
+
+    def load(t):
+        first_bin = pl.multiple_of(meet(s, t, ns) * bins, bins)
+        return pltpu.make_async_copy(spectra_ref.at[:, :, pl.ds(first_bin, bins), :], raw_ref.at[t], load_sem.at[t])
+
+    def ready(t):
+        load(t).wait()
+        prepare(t, meet(s, t, ns), raw_ref, weight_ref, wide_ref, x_ref)
+
+    if fused:
+        for t in range(ns):
+            load(t).start()
+        lax.fori_loop(0, min(2, ns), lambda t, carry: (ready(t), carry)[1], 0)
 
     pl.semaphore_wait(barrier, ns - 1 + has_up.astype(jnp.int32) + has_down.astype(jnp.int32))
 
@@ -90,6 +118,11 @@
         down(p, s, x_ref.at[s]).start()
 
     def send(t, carry):
+        if fused:
+            @pl.when(t + 1 < ns)
+            def _():
+                ready(t + 1)
+
         exchange(t).start()
         return carry
 
@@ -253,20 +286,30 @@
 def shards(ns, np_, spectra, shot_weight):
     _, depth, freqs, width = spectra.shape
     bins = freqs // ns
-    scaled = (spectra.astype(jnp.float32) * shot_weight[None, :, None, None]).astype(jnp.bfloat16)
-    outgoing = scaled.transpose(2, 0, 1, 3).reshape(ns, bins, 2, depth, width)
     factor = (depth * ns) ** -0.5
-    fused = width % 128 == 0
+    fused = width % 128 == 0 and bins % 16 == 0 and depth % 16 == 0
     shapes = [(np_, ns, bins, 2, depth, width)]
     if fused:
         shapes += [(bins, 2 * width, ns * 2 * depth), (2, bins, width, np_ * width)]
+        operands = tuple(pltpu.with_memory_space_constraint(a, pltpu.HBM) for a in (spectra, shot_weight))
+        in_specs = [pl.BlockSpec(memory_space=pltpu.HBM), pl.BlockSpec(memory_space=pltpu.SMEM)]
+        scratch = [
+            pltpu.VMEM((ns, bins, 2, depth, width), jnp.bfloat16),
+            pltpu.VMEM((ns, 2, depth, bins, width), jnp.bfloat16),
+            pltpu.VMEM((width // 128, 2 * depth * bins, 128), jnp.float32),
+            pltpu.SemaphoreType.DMA((ns,)),
+        ]
+    else:
+        scaled = (spectra.astype(jnp.float32) * shot_weight[None, :, None, None]).astype(jnp.bfloat16)
+        operands = (scaled.transpose(2, 0, 1, 3).reshape(ns, bins, 2, depth, width),)
+        in_specs, scratch = [pl.BlockSpec(memory_space=pl.ANY)], []
     place = pltpu.VMEM if fused else pl.ANY
     results = pl.pallas_call(
         functools.partial(gather_kernel, ns, np_, factor, fused),
         out_shape=[pltpu.VMEM(n, jnp.bfloat16) if fused else jax.ShapeDtypeStruct(n, jnp.bfloat16) for n in shapes],
-        in_specs=[pl.BlockSpec(memory_space=pl.ANY)],
+        in_specs=in_specs,
         out_specs=[pl.BlockSpec(memory_space=place)] * len(shapes),
-        scratch_shapes=[
+        scratch_shapes=scratch + [
             pltpu.SemaphoreType.DMA((ns,)),
             pltpu.SemaphoreType.DMA((np_, ns)),
             pltpu.SemaphoreType.DMA((np_, ns)),
@@ -275,7 +318,7 @@
         ],
         compiler_params=pltpu.CompilerParams(
             collective_id=0, has_side_effects=True, vmem_limit_bytes=16 * 2**20),
-    )(outgoing)
+    )(*operands)
     if fused:
         return finish(np_, factor, *results)
     return gram(results[0], factor)

time: 154 us -> 151 us (0.981)
  other arithmetic: 2.62 us -> 0 us
    transpose x1 -> x0, other arithmetic: 2.62 us -> none  [shards(): outgoing = scaled.transpose(2, 0, 1, 3).reshape(ns, bins, 2, depth, width)]
where the time goes in v3:
time: 151 us; the launch traced here: 150 us
  Pallas kernels  150 us (99%)
    pallas_call x1, Pallas kernels, shards(): pl.pallas_call(functools.partial(gather_kernel, ns, np_, factor, fused),...  144 us
    pallas_call x1, Pallas kernels, finish(): pl.pallas_call(functools.partial(finish_kernel, np_, factor), out_shape=j...  6.09 us

profile of v3, /device:TPU:0, one launch (start us, length us, event | category | flops | bytes accessed | tf_op | source)
XLA Modules:
  0.0 150.4 jit_solution(1174414258694114950)
XLA Ops:
  0.0 144.3 %shard_map.28 = (bf16[4,8,16,2,16,256]{5,4,3,2,1,0:T(8,128)(2,1)S(1)}, bf16[16,512,256]{2,1,0:T(8,128)(2,1)S(1)}, bf16[2,16,256,1024]{3,2,1,0:T(8,128)(2,1)S(1)}) custom-call(bf16[2,16,128,256]{3,2,1,0:T(8,128)(2,1)} %refs_0_.1, f32[16]{0:T(128)} %refs_1_.1), custom_call_target="tpu_custom_call" | custom-call | tf_op jit(solution)/shard_map/pallas_call | solution.py:307
  144.3 6.1 %shard_map.29 = bf16[2,16,256,1024]{3,2,1,0:T(8,128)(2,1)} custom-call(bf16[4,8,16,2,16,256]{5,4,3,2,1,0:T(8,128)(2,1)S(1)} %get-tuple-element.8.g_ref, bf16[16,512,256]{2,1,0:T(8,128)(2,1)S(1)} %get-tuple-element.9.left_ref, bf16[2,16,256,1024]{3,2,1,0:T(8,128)(2,1)S(1)} %get-tuple-element.10.o_ref), custom_call_target="tpu_custom_call" | custom-call | tf_op jit(solution)/shard_map/pallas_call | solution.py:264

commit v4 on v3

--- a/solution.py
+++ b/solution.py
@@ -48,7 +48,7 @@
 
 def gather_kernel(ns, np_, factor, fused, *refs):
     if fused:
-        spectra_ref, weight_ref, g_ref, left_ref, o_ref, x_ref, raw_ref, wide_ref, load_sem, *sems = refs
+        spectra_ref, shot_weight_ref, g_ref, left_ref, o_ref, x_ref, raw_ref, wide_ref, weight_ref, load_sem, weight_sem, *sems = refs
     else:
         x_ref, g_ref, *sems = refs
     a2a_sem, up_sem, down_sem, recv_sem, own_sem = sems
@@ -57,33 +57,39 @@
     share = -(-bins // ns)
     has_up, has_down = p < np_ - 1, p > 0
 
-    barrier = pltpu.get_barrier_semaphore()
-
-    def hello(t, carry):
-        pl.semaphore_signal(barrier, inc=1, device_id=(meet(s, t, ns), p), device_id_type=MESH)
-        return carry
-
-    lax.fori_loop(1, ns, hello, 0)
-
-    @pl.when(has_up)
-    def _():
-        pl.semaphore_signal(barrier, inc=1, device_id=(s, p + 1), device_id_type=MESH)
-
-    @pl.when(has_down)
-    def _():
-        pl.semaphore_signal(barrier, inc=1, device_id=(s, p - 1), device_id_type=MESH)
-
     def load(t):
         first_bin = pl.multiple_of(meet(s, t, ns) * bins, bins)
         return pltpu.make_async_copy(spectra_ref.at[:, :, pl.ds(first_bin, bins), :], raw_ref.at[t], load_sem.at[t])
 
+    if fused:
+        weights = pltpu.make_async_copy(shot_weight_ref, weight_ref, weight_sem)
+        load(0).start()
+        weights.start()
+        for t in range(1, ns):
+            load(t).start()
+
+    barrier = pltpu.get_barrier_semaphore()
+
+    def hello(t, carry):
+        pl.semaphore_signal(barrier, inc=1, device_id=(meet(s, t, ns), p), device_id_type=MESH)
+        return carry
+
+    lax.fori_loop(1, ns, hello, 0)
+
+    @pl.when(has_up)
+    def _():
+        pl.semaphore_signal(barrier, inc=1, device_id=(s, p + 1), device_id_type=MESH)
+
+    @pl.when(has_down)
+    def _():
+        pl.semaphore_signal(barrier, inc=1, device_id=(s, p - 1), device_id_type=MESH)
+
     def ready(t):
         load(t).wait()
         prepare(t, meet(s, t, ns), raw_ref, weight_ref, wide_ref, x_ref)
 
     if fused:
-        for t in range(ns):
-            load(t).start()
+        weights.wait()
         lax.fori_loop(0, min(2, ns), lambda t, carry: (ready(t), carry)[1], 0)
 
     pl.semaphore_wait(barrier, ns - 1 + has_up.astype(jnp.int32) + has_down.astype(jnp.int32))
@@ -147,6 +153,21 @@
 
     own.wait()
 
+    def exchanged(t, carry):
+        exchange(t).wait_send()
+        return carry
+
+    lax.fori_loop(1, ns, exchanged, 0)
+
+    def collect(r, j):
+        @pl.when(has_up & (p >= r))
+        def _():
+            up(p - r, j, g_ref.at[p - r, j]).wait_send()
+
+        @pl.when(has_down & (p + r < np_))
+        def _():
+            down(p + r, j, g_ref.at[p + r, j]).wait_send()
+
     def multiply(f, q):
         product = block_product(f, q, g_ref, left_ref, factor)
         columns = pl.ds(pl.multiple_of(q * width, width), width)
@@ -174,49 +195,38 @@
 
     def relay(i, carry):
         r, j = i // ns, meet(s, i % ns, ns)
-
-        @pl.when(p >= r)
-        def _():
-            arrived(p - r, j)
-
-            @pl.when(has_up)
-            def _():
-                up(p - r, j, g_ref.at[p - r, j]).start()
-
-        @pl.when(p + r < np_)
-        def _():
-            arrived(p + r, j)
-
-            @pl.when(has_down)
-            def _():
-                down(p + r, j, g_ref.at[p + r, j]).start()
-
         if fused:
             compute(r - 1, i % ns)
+
+        @pl.when(r > 1)
+        def _():
+            collect(r - 2, j)
+
+        @pl.when(p >= r)
+        def _():
+            arrived(p - r, j)
+
+            @pl.when(has_up)
+            def _():
+                up(p - r, j, g_ref.at[p - r, j]).start()
+
+        @pl.when(p + r < np_)
+        def _():
+            arrived(p + r, j)
+
+            @pl.when(has_down)
+            def _():
+                down(p + r, j, g_ref.at[p + r, j]).start()
+
         return carry
 
     lax.fori_loop(ns, np_ * ns, relay, 0)
 
-    def exchanged(t, carry):
-        exchange(t).wait_send()
-        return carry
-
-    lax.fori_loop(1, ns, exchanged, 0)
-
-    def sent(i, carry):
-        q, j = i // ns, i % ns
-
-        @pl.when(has_up & (q <= p))
-        def _():
-            up(q, j, g_ref.at[q, j]).wait_send()
-
-        @pl.when(has_down & (q >= p))
-        def _():
-            down(q, j, g_ref.at[q, j]).wait_send()
-
-        return carry
-
-    lax.fori_loop(0, np_ * ns, sent, 0)
+    def rest(i, carry):
+        collect(i // ns, i % ns)
+        return carry
+
+    lax.fori_loop(max(np_ - 2, 0) * ns, np_ * ns, rest, 0)
 
 
 def finish_kernel(np_, factor, g_ref, left_ref, o_ref, out_ref, last_ref, done_sem, last_sem):
@@ -292,12 +302,14 @@
     if fused:
         shapes += [(bins, 2 * width, ns * 2 * depth), (2, bins, width, np_ * width)]
         operands = tuple(pltpu.with_memory_space_constraint(a, pltpu.HBM) for a in (spectra, shot_weight))
-        in_specs = [pl.BlockSpec(memory_space=pltpu.HBM), pl.BlockSpec(memory_space=pltpu.SMEM)]
+        in_specs = [pl.BlockSpec(memory_space=pltpu.HBM), pl.BlockSpec(memory_space=pltpu.HBM)]
         scratch = [
             pltpu.VMEM((ns, bins, 2, depth, width), jnp.bfloat16),
             pltpu.VMEM((ns, 2, depth, bins, width), jnp.bfloat16),
             pltpu.VMEM((width // 128, 2 * depth * bins, 128), jnp.float32),
+            pltpu.SMEM((depth,), jnp.float32),
             pltpu.SemaphoreType.DMA((ns,)),
+            pltpu.SemaphoreType.DMA,
         ]
     else:
         scaled = (spectra.astype(jnp.float32) * shot_weight[None, :, None, None]).astype(jnp.bfloat16)

time: 151 us -> 149 us (0.987)
    pallas_call x1, Pallas kernels: 144 us -> 142 us  [shards(): pl.pallas_call(functools.partial(gather_kernel, ns, np_, factor, fused),...]
where the time goes in v4:
time: 149 us
  Pallas kernels  149 us (100%)
    pallas_call x1, Pallas kernels, shards(): pl.pallas_call(functools.partial(gather_kernel, ns, np_, factor, fused),...  142 us
    pallas_call x1, Pallas kernels, finish(): pl.pallas_call(functools.partial(finish_kernel, np_, factor), out_shape=j...  6.09 us

profile of v4, /device:TPU:0, one launch (start us, length us, event | category | flops | bytes accessed | tf_op | source)
XLA Modules:
  0.0 148.6 jit_solution(15738054594840196630)
XLA Ops:
  0.0 142.5 %shard_map.28 = (bf16[4,8,16,2,16,256]{5,4,3,2,1,0:T(8,128)(2,1)S(1)}, bf16[16,512,256]{2,1,0:T(8,128)(2,1)S(1)}, bf16[2,16,256,1024]{3,2,1,0:T(8,128)(2,1)S(1)}) custom-call(bf16[2,16,128,256]{3,2,1,0:T(8,128)(2,1)} %refs_0_.1, f32[16]{0:T(128)} %refs_1_.1), custom_call_target="tpu_custom_call" | custom-call | tf_op jit(solution)/shard_map/pallas_call | solution.py:319
  142.5 6.1 %shard_map.29 = bf16[2,16,256,1024]{3,2,1,0:T(8,128)(2,1)} custom-call(bf16[4,8,16,2,16,256]{5,4,3,2,1,0:T(8,128)(2,1)S(1)} %get-tuple-element.8.g_ref, bf16[16,512,256]{2,1,0:T(8,128)(2,1)S(1)} %get-tuple-element.9.left_ref, bf16[2,16,256,1024]{3,2,1,0:T(8,128)(2,1)S(1)} %get-tuple-element.10.o_ref), custom_call_target="tpu_custom_call" | custom-call | tf_op jit(solution)/shard_map/pallas_call | solution.py:274

commit v5 on v4

--- a/solution.py
+++ b/solution.py
@@ -32,13 +32,17 @@
     return (jnp.dot(left_ref[f], right, preferred_element_type=jnp.float32) * factor).astype(jnp.bfloat16)
 
 
-def prepare(t, j, raw_ref, weight_ref, wide_ref, x_ref):
+def widen(t, raw_ref, weight_ref, wide_ref):
     _, _, depth, bins, width = raw_ref.shape
     for c in range(2):
         for k in range(depth):
             scaled = raw_ref[t, c, k].astype(jnp.float32) * weight_ref[k]
             for h in range(width // 128):
                 wide_ref[h, pl.ds((c * depth + k) * bins, bins), :] = scaled[:, h * 128:(h + 1) * 128]
+
+
+def narrow(j, wide_ref, x_ref):
+    _, bins, _, depth, width = x_ref.shape
     for c in range(2):
         for f in range(bins):
             for h in range(width // 128):
@@ -86,11 +90,15 @@
 
     def ready(t):
         load(t).wait()
-        prepare(t, meet(s, t, ns), raw_ref, weight_ref, wide_ref, x_ref)
+        widen(t, raw_ref, weight_ref, wide_ref)
+        narrow(meet(s, t, ns), wide_ref, x_ref)
 
     if fused:
         weights.wait()
-        lax.fori_loop(0, min(2, ns), lambda t, carry: (ready(t), carry)[1], 0)
+        ready(0)
+        if ns > 1:
+            load(1).wait()
+            widen(1, raw_ref, weight_ref, wide_ref)
 
     pl.semaphore_wait(barrier, ns - 1 + has_up.astype(jnp.int32) + has_down.astype(jnp.int32))
 
@@ -122,6 +130,9 @@
     @pl.when(has_down)
     def _():
         down(p, s, x_ref.at[s]).start()
+
+    if fused and ns > 1:
+        narrow(meet(s, 1, ns), wide_ref, x_ref)
 
     def send(t, carry):
         if fused:

time: 149 us -> 149 us (level)
  no operation moved by 1% of the time
where the time goes in v5:
time: 149 us
  Pallas kernels  149 us (100%)
    pallas_call x1, Pallas kernels, shards(): pl.pallas_call(functools.partial(gather_kernel, ns, np_, factor, fused),...  142 us
    pallas_call x1, Pallas kernels, finish(): pl.pallas_call(functools.partial(finish_kernel, np_, factor), out_shape=j...  6.09 us

profile of v5, /device:TPU:0, one launch (start us, length us, event | category | flops | bytes accessed | tf_op | source)
XLA Modules:
  0.0 148.6 jit_solution(6273244716539735175)
XLA Ops:
  0.0 142.5 %shard_map.28 = (bf16[4,8,16,2,16,256]{5,4,3,2,1,0:T(8,128)(2,1)S(1)}, bf16[16,512,256]{2,1,0:T(8,128)(2,1)S(1)}, bf16[2,16,256,1024]{3,2,1,0:T(8,128)(2,1)S(1)}) custom-call(bf16[2,16,128,256]{3,2,1,0:T(8,128)(2,1)} %refs_0_.1, f32[16]{0:T(128)} %refs_1_.1), custom_call_target="tpu_custom_call" | custom-call | tf_op jit(solution)/shard_map/pallas_call | solution.py:330
  142.5 6.1 %shard_map.29 = bf16[2,16,256,1024]{3,2,1,0:T(8,128)(2,1)} custom-call(bf16[4,8,16,2,16,256]{5,4,3,2,1,0:T(8,128)(2,1)S(1)} %get-tuple-element.8.g_ref, bf16[16,512,256]{2,1,0:T(8,128)(2,1)S(1)} %get-tuple-element.9.left_ref, bf16[2,16,256,1024]{3,2,1,0:T(8,128)(2,1)S(1)} %get-tuple-element.10.o_ref), custom_call_target="tpu_custom_call" | custom-call | tf_op jit(solution)/shard_map/pallas_call | solution.py:285
